TPU v7x, 512 devices: a whole 4x4x16 slice. The times are simulated.
512 devices in a mesh: term: 8 (over y, core), doc: 16 (over z), enc: 4 (over x).
Axes of the slice: x: 4, y: 4, z: 16, core: 2. Of those that a mesh axis runs over, the one named last changes fastest.
Arguments:
- query_weights: bfloat16 [1024, 30720], P('enc', ('term', 'doc')), may hold values from 0.049804688 to 2
- tile_terms: int32 [30720], P(('term', 'doc')), may hold values from 0 to 59
- tile_blocks: int32 [30720], P(('term', 'doc')), may hold values from 0 to 15
- tile_counts: int32 [128], P(('term', 'doc')), may hold values from 60 to 240, as said below
- impacts: bfloat16 [30720, 64, 128], P(('term', 'doc')), may hold values from -0.015625 to 0.015625
Outputs:
- scores: float32 [2048, 1024], P('doc', 'enc')
Inputs may be any that keep to these rules, and one draw needn't show every extreme that they name: Slots at positions tile_counts or later of a device's list are padding and contribute nothing; some device has all 240 slots live.
All inputs are finite; a program needn't handle non-finite values.
Results may differ from a plain program's by a relative error of at most 0.0003.
Values may be sent and summed in bfloat16 or wider, within the bound.
No kernel may reach another device: no remote copies, remote signals or barrier semaphores. Data moves between devices by JAX's collectives and lax.ppermute only.
A program may use at most 64 MiB of HBM per device.

v0:
```python
import jax
import jax.numpy as jnp
from jax import lax
from jax.sharding import PartitionSpec as P


def block_size(tiles):
    largest = 1
    for divisor in range(1, 65):
        if tiles % divisor == 0:
            largest = divisor
    return largest


def per_device(query_weights, tile_terms, tile_blocks, tile_counts, impacts):
    range_rows = lax.all_gather(query_weights, "doc", axis=1, tiled=True)
    queries = range_rows.shape[0]
    tiles, term_block, doc_block = impacts.shape
    owners = lax.axis_size("doc")
    grouped = range_rows.reshape(queries, range_rows.shape[1] // term_block, term_block)
    step = block_size(tiles)
    live = jnp.arange(tiles, dtype=jnp.int32) < tile_counts[0]
    owner_ids = jnp.arange(owners, dtype=jnp.int32)

    def accumulate(total, number):
        start = number * step
        term_now = lax.dynamic_slice_in_dim(tile_terms, start, step)
        owner_now = lax.dynamic_slice_in_dim(tile_blocks, start, step)
        keep_now = lax.dynamic_slice_in_dim(live, start, step)
        tile_now = lax.dynamic_slice_in_dim(impacts, start, step)
        picked = jnp.take(grouped, term_now, axis=1)
        product = jnp.einsum("qnk,nkd->ndq", picked, tile_now, preferred_element_type=jnp.float32)
        select = ((owner_now[:, None] == owner_ids[None, :]) & keep_now[:, None]).astype(
            jnp.float32
        )
        added = jnp.einsum("ndq,nb->bdq", product, select, precision=lax.Precision.HIGHEST)
        return (total + added, None)

    start_total = jnp.zeros((owners, doc_block, queries), jnp.float32)
    total, unused = lax.scan(accumulate, start_total, jnp.arange(tiles // step, dtype=jnp.int32))
    partial_value = total.reshape(owners * doc_block, queries)
    mine = lax.psum_scatter(partial_value, "doc", scatter_dimension=0, tiled=True)
    scores = lax.psum(mine, "term")
    return scores


def solution(mesh):
    return jax.shard_map(
        per_device,
        mesh=mesh,
        in_specs=(
            P("enc", ("term", "doc")),
            P(("term", "doc")),
            P(("term", "doc")),
            P(("term", "doc")),
            P(("term", "doc"), None, None),
        ),
        out_specs=P("doc", "enc"),
        check_vma=False,
    )
```

profile of v0, /device:TPU:2, one launch (start us, length us, event | category | flops | bytes accessed | tf_op | source)
XLA Modules:
  0.0 312.8 jit_solution(1491762189442942286)
XLA Ops:
  6.5 0.7 all-gather.2.cloned.1.call-update
  8.0 78.3 %all-gather.2.cloned.1.call-done = bf16[256,3840]{0,1:T(8,128)(2,1)} async-done(((bf16[256,240]{0,1:T(8,128)(2,1)}), bf16[256,3840]{0,1:T(8,128)(2,1)}) %all-gather.2.cloned.1.call-update) | async-done | bytes 1966096 | tf_op jit(solution)/shard_map/all_gather | solution.py:16
  86.2 67.8 %while.11 = (s32[]{:T(128)}, f32[16,128,256]{2,0,1:T(8,128)}, s32[4]{0:T(128)S(1)}, s32[240]{0:T(256)}, pred[240]{0:T(512)(128)(4,1)S(1)}, /*index=5*/bf16[240,6...) while((s32[]{:T(128)}, f32[16,128,256]{2,0,1:T(8,128)}, ...), condition=%wide.region_1.2_spmd.clone, body=%wide.region_0.1_spmd.clone.sunk | while | flops 631180544 | bytes 43587780 | solution.py:40
  86.2 0.6 dynamic_slice.30
  87.6 0.8 dynamic_slice.31
  88.3 0.8 compare_and_fusion.2
  89.1 2.2 gather_fusion
  91.3 2.6 fusion.28
  93.9 7.9 %select_add_fusion.2 = f32[16,128,256]{2,0,1:T(8,128)S(1)} fusion(f32[16,128,256]{2,0,1:T(8,128)S(1)} %copy-done, f32[60,128,256]{2,1,0:T(8,128)S(1)} %fusion.28, pred[]{:T(512)S(6)} %compare.3, s32[60]{0:T(128)S(1)} %dynamic_slice.31, pred[60]{0:T(512)(128)(4,1)S(1)} %dynamic_slice.32), kind=kOutput, calls=%fused_computation.4.clone.1 | convolution fusion | flops 378537856 | bytes 12058925 | tf_op jit(solution)/shard_map/while/body/eval_jaxpr/ndq,nb->bdq/dot_general | solution.py:36
  101.9 1.3 copy-done.1
  104.5 0.8 dynamic_slice.31
  105.2 0.8 compare_and_fusion.2
  106.0 2.2 gather_fusion
  108.3 2.6 fusion.28
  110.9 7.9 %select_add_fusion.2 = f32[16,128,256]{2,0,1:T(8,128)S(1)} fusion(f32[16,128,256]{2,0,1:T(8,128)S(1)} %copy-done, f32[60,128,256]{2,1,0:T(8,128)S(1)} %fusion.28, pred[]{:T(512)S(6)} %compare.3, s32[60]{0:T(128)S(1)} %dynamic_slice.31, pred[60]{0:T(512)(128)(4,1)S(1)} %dynamic_slice.32), kind=kOutput, calls=%fused_computation.4.clone.1 | convolution fusion | flops 378537856 | bytes 12058925 | tf_op jit(solution)/shard_map/while/body/eval_jaxpr/ndq,nb->bdq/dot_general | solution.py:36
  118.8 1.3 copy-done.1
  121.4 0.8 dynamic_slice.31
  122.2 0.8 compare_and_fusion.2
  122.9 2.2 gather_fusion
  125.2 2.6 fusion.28
  127.8 7.9 %select_add_fusion.2 = f32[16,128,256]{2,0,1:T(8,128)S(1)} fusion(f32[16,128,256]{2,0,1:T(8,128)S(1)} %copy-done, f32[60,128,256]{2,1,0:T(8,128)S(1)} %fusion.28, pred[]{:T(512)S(6)} %compare.3, s32[60]{0:T(128)S(1)} %dynamic_slice.31, pred[60]{0:T(512)(128)(4,1)S(1)} %dynamic_slice.32), kind=kOutput, calls=%fused_computation.4.clone.1 | convolution fusion | flops 378537856 | bytes 12058925 | tf_op jit(solution)/shard_map/while/body/eval_jaxpr/ndq,nb->bdq/dot_general | solution.py:36
  135.7 1.3 copy-done.1
  138.4 0.8 dynamic_slice.31
  139.1 0.8 compare_and_fusion.2
  139.9 2.2 gather_fusion
  142.1 2.6 fusion.28
  144.8 7.9 %select_add_fusion.2 = f32[16,128,256]{2,0,1:T(8,128)S(1)} fusion(f32[16,128,256]{2,0,1:T(8,128)S(1)} %copy-done, f32[60,128,256]{2,1,0:T(8,128)S(1)} %fusion.28, pred[]{:T(512)S(6)} %compare.3, s32[60]{0:T(128)S(1)} %dynamic_slice.31, pred[60]{0:T(512)(128)(4,1)S(1)} %dynamic_slice.32), kind=kOutput, calls=%fused_computation.4.clone.1 | convolution fusion | flops 378537856 | bytes 12058925 | tf_op jit(solution)/shard_map/while/body/eval_jaxpr/ndq,nb->bdq/dot_general | solution.py:36
  152.7 1.3 copy-done.1
  154.0 4.1 %copy.8 = f32[16,128,256]{2,1,0:T(8,128)} copy(f32[16,128,256]{2,0,1:T(8,128)} %get-tuple-element.52) | data formatting | bytes 4194304 | tf_op jit(solution)/shard_map/while | solution.py:40
  158.2 71.0 %reduce-scatter.2.cloned.1.call-done = f32[128,256]{1,0:T(8,128)} async-done(((f32[2048,256]{1,0:T(8,128)}), f32[128,256]{1,0:T(8,128)}) %reduce-scatter.2.cloned.1.call-update) | async-done | bytes 131088 | tf_op jit(solution)/shard_map/reduce_scatter | solution.py:42
  229.3 75.4 %all-reduce.2.cloned.1.call-done = f32[128,256]{1,0:T(8,128)} async-done(((f32[128,256]{1,0:T(8,128)}), f32[128,256]{1,0:T(8,128)}) %all-reduce.2.cloned.1.call-update) | async-done | bytes 131088 | tf_op jit(solution)/shard_map/psum | solution.py:43
  304.7 1.6 copy.24
  (31 shorter events, 2.3 us)
Async XLA Ops:
  6.5 79.7 %all-gather.2.cloned.1.call-start = ((), (), s32[]{:S(2)}) async-start(), calls=%async_computation.1 | async-start | bytes 2088960 | tf_op jit(solution)/shard_map/all_gather | solution.py:16
  7.3 222.0 %reduce-scatter.2.cloned.1.call-start = ((), (), s32[]{:S(2)}) async-start(), calls=%async_computation.2 | async-start | bytes 2228224 | tf_op jit(solution)/shard_map/reduce_scatter | solution.py:42
  91.3 2.6 copy-start
  101.8 1.3 copy-start.1
  108.2 2.6 copy-start
  118.8 1.3 copy-start.1
  125.2 2.6 copy-start
  135.7 1.3 copy-start.1
  142.1 2.6 copy-start
  152.7 1.3 copy-start.1
  158.2 146.6 %all-reduce.2.cloned.1.call-start = ((), (), s32[]{:S(2)}) async-start(), calls=%async_computation.3 | async-start | bytes 262144 | tf_op jit(solution)/shard_map/psum | solution.py:43
Sparse Core Ops, SparseCore 0:
  9.4 76.7 all-gather.1
  158.3 70.9 reduce-scatter.1
  231.6 73.0 all-reduce.1
where the time goes:
time: 313 us
  waiting for transfers between devices  225 us (72%)
  matrix products  42 us (13%)
  local copies, waits for them, and re-layouts  25.7 us (8%)
  between operations  13.8 us (4%)
    all_gather x1, waiting for transfers between devices, per_device(): range_rows = lax.all_gather(query_weights, 'doc', axis=1, tiled=True)  78.3 us
    psum x1, waiting for transfers between devices, per_device(): scores = lax.psum(mine, 'term')  75.4 us
    reduce_scatter x1, waiting for transfers between devices, per_device(): lax.psum_scatter(partial_value, 'doc', scatter_dimension=0, tiled=True)  71 us
    dot_general x4, matrix products, accumulate(): jnp.einsum('ndq,nb->bdq', product, select, precision=lax.Precision.HIGHEST)  31.6 us
    dot_general x4, matrix products, accumulate(): jnp.einsum('qnk,nkd->ndq', picked, tile_now, preferred_element_type=jnp.f...  10.5 us
    gather x4, local copies, waits for them, and re-layouts, accumulate(): picked = jnp.take(grouped, term_now, axis=1)  8.92 us
  transfers between devices with their start and end apart: 3, of which 3 were waited for; matrix products, arithmetic and copies ran while one was open for 0% of the time, Pallas kernels for 0%

commit v1 on v0

--- a/solution.py
+++ b/solution.py
@@ -40,7 +40,9 @@
     total, unused = lax.scan(accumulate, start_total, jnp.arange(tiles // step, dtype=jnp.int32))
     partial_value = total.reshape(owners * doc_block, queries)
     mine = lax.psum_scatter(partial_value, "doc", scatter_dimension=0, tiled=True)
-    scores = lax.psum(mine, "term")
+    scores = mine
+    for hop in (1, 2, 4):
+        scores = scores + lax.ppermute(scores, "term", [(dev, dev ^ hop) for dev in range(8)])
     return scores
 
 

time: 313 us -> 257 us (0.82)
  waiting for transfers between devices: 225 us -> 159 us
  starting transfers between devices: 0.08 us -> 9.99 us
    psum x1 -> x0, waiting for transfers between devices: 75.4 us -> none  [per_device(): scores = lax.psum(mine, 'term')]
    ppermute x0 -> x3, starting transfers between devices: none -> 9.95 us  [per_device(): lax.ppermute(scores, 'term', [(dev, dev ^ hop) for dev in range(8)])]
    ppermute x0 -> x3, waiting for transfers between devices: none -> 9.28 us  [per_device(): lax.ppermute(scores, 'term', [(dev, dev ^ hop) for dev in range(8)])]
  transfers between devices with their start and end apart: 3 -> 5, of which waited for: 3 -> 5; matrix products, arithmetic and copies ran while one was open for 0% -> 0% of each run, Pallas kernels for 0% -> 0%
where the time goes in v1:
time: 257 us
  waiting for transfers between devices  159 us (62%)
  matrix products  42 us (16%)
  local copies, waits for them, and re-layouts  24 us (9%)
  between operations  14.1 us (5%)
  starting transfers between devices  9.99 us (4%)
  other arithmetic  4.67 us (2%)
    all_gather x1, waiting for transfers between devices, per_device(): range_rows = lax.all_gather(query_weights, 'doc', axis=1, tiled=True)  78.3 us
    reduce_scatter x1, waiting for transfers between devices, per_device(): lax.psum_scatter(partial_value, 'doc', scatter_dimension=0, tiled=True)  71.2 us
    dot_general x4, matrix products, accumulate(): jnp.einsum('ndq,nb->bdq', product, select, precision=lax.Precision.HIGHEST)  31.6 us
    dot_general x4, matrix products, accumulate(): jnp.einsum('qnk,nkd->ndq', picked, tile_now, preferred_element_type=jnp.f...  10.5 us
    ppermute x3, starting transfers between devices, per_device(): lax.ppermute(scores, 'term', [(dev, dev ^ hop) for dev in range(8)])  9.95 us
    ppermute x3, waiting for transfers between devices, per_device(): lax.ppermute(scores, 'term', [(dev, dev ^ hop) for dev in range(8)])  9.28 us
    gather x4, local copies, waits for them, and re-layouts, accumulate(): picked = jnp.take(grouped, term_now, axis=1)  8.92 us
    while x16, local copies, waits for them, and re-layouts  5.32 us
  transfers between devices with their start and end apart: 5, of which 5 were waited for; matrix products, arithmetic and copies ran while one was open for 0% of the time, Pallas kernels for 0%

profile of v1, /device:TPU:2, one launch (start us, length us, event | category | flops | bytes accessed | tf_op | source)
XLA Modules:
  0.0 256.7 jit_solution(13428880006579317802)
XLA Ops:
  8.0 78.3 %all-gather.2.cloned.1.call-done = bf16[256,3840]{0,1:T(8,128)(2,1)} async-done(((bf16[256,240]{0,1:T(8,128)(2,1)}), bf16[256,3840]{0,1:T(8,128)(2,1)}) %all-gather.2.cloned.1.call-update) | async-done | bytes 1966096 | tf_op jit(solution)/shard_map/all_gather | solution.py:16
  86.2 67.4 %while.11 = (s32[]{:T(128)}, f32[16,128,256]{2,0,1:T(8,128)}, s32[4]{0:T(128)S(1)}, s32[240]{0:T(256)}, pred[240]{0:T(512)(128)(4,1)S(1)}, /*index=5*/bf16[240,6...) while((s32[]{:T(128)}, f32[16,128,256]{2,0,1:T(8,128)}, ...), condition=%wide.region_1.2_spmd.clone, body=%wide.region_0.1_spmd.clone.sunk | while | flops 631180544 | bytes 43587780 | solution.py:40
  87.5 0.8 dynamic_slice.31
  88.2 0.8 compare_and_fusion.2
  89.0 2.2 gather_fusion
  91.2 2.6 %fusion.28 = f32[60,128,256]{2,1,0:T(8,128)S(1)} fusion(bf16[60,256,64]{1,2,0:T(8,128)(2,1)S(1)} %gather_fusion, pred[60]{0:T(512)(128)(4,1)S(1)} %get-tuple-element.152, bf16[240,64,128]{2,1,0:T(8,128)(2,1)} %get-tuple-element.182, s32[]{:T(128)S(6)} %select_n.28), kind=kOutput, calls=%fused_computation.5.clone.1 | convolution fusion | flops 252641280 | bytes 10813504 | tf_op jit(solution)/shard_map/while/body/eval_jaxpr/qnk,nkd->ndq/dot_general | solution.py:32
  93.9 7.9 %select_add_fusion.2 = f32[16,128,256]{2,0,1:T(8,128)S(1)} fusion(f32[16,128,256]{2,0,1:T(8,128)S(1)} %copy-done, f32[60,128,256]{2,1,0:T(8,128)S(1)} %fusion.28, pred[]{:T(512)S(6)} %compare.3, s32[60]{0:T(128)S(1)} %dynamic_slice.31, pred[60]{0:T(512)(128)(4,1)S(1)} %dynamic_slice.32), kind=kOutput, calls=%fused_computation.4.clone.1 | convolution fusion | flops 378537856 | bytes 12058925 | tf_op jit(solution)/shard_map/while/body/eval_jaxpr/ndq,nb->bdq/dot_general | solution.py:36
  101.8 1.3 copy-done.1
  105.1 0.8 compare_and_fusion.2
  105.9 2.2 gather_fusion
  108.1 2.6 %fusion.28 = f32[60,128,256]{2,1,0:T(8,128)S(1)} fusion(bf16[60,256,64]{1,2,0:T(8,128)(2,1)S(1)} %gather_fusion, pred[60]{0:T(512)(128)(4,1)S(1)} %get-tuple-element.152, bf16[240,64,128]{2,1,0:T(8,128)(2,1)} %get-tuple-element.182, s32[]{:T(128)S(6)} %select_n.28), kind=kOutput, calls=%fused_computation.5.clone.1 | convolution fusion | flops 252641280 | bytes 10813504 | tf_op jit(solution)/shard_map/while/body/eval_jaxpr/qnk,nkd->ndq/dot_general | solution.py:32
  110.7 7.9 %select_add_fusion.2 = f32[16,128,256]{2,0,1:T(8,128)S(1)} fusion(f32[16,128,256]{2,0,1:T(8,128)S(1)} %copy-done, f32[60,128,256]{2,1,0:T(8,128)S(1)} %fusion.28, pred[]{:T(512)S(6)} %compare.3, s32[60]{0:T(128)S(1)} %dynamic_slice.31, pred[60]{0:T(512)(128)(4,1)S(1)} %dynamic_slice.32), kind=kOutput, calls=%fused_computation.4.clone.1 | convolution fusion | flops 378537856 | bytes 12058925 | tf_op jit(solution)/shard_map/while/body/eval_jaxpr/ndq,nb->bdq/dot_general | solution.py:36
  118.6 1.3 copy-done.1
  122.0 0.8 compare_and_fusion.2
  122.7 2.2 gather_fusion
  125.0 2.6 %fusion.28 = f32[60,128,256]{2,1,0:T(8,128)S(1)} fusion(bf16[60,256,64]{1,2,0:T(8,128)(2,1)S(1)} %gather_fusion, pred[60]{0:T(512)(128)(4,1)S(1)} %get-tuple-element.152, bf16[240,64,128]{2,1,0:T(8,128)(2,1)} %get-tuple-element.182, s32[]{:T(128)S(6)} %select_n.28), kind=kOutput, calls=%fused_computation.5.clone.1 | convolution fusion | flops 252641280 | bytes 10813504 | tf_op jit(solution)/shard_map/while/body/eval_jaxpr/qnk,nkd->ndq/dot_general | solution.py:32
  127.6 7.9 %select_add_fusion.2 = f32[16,128,256]{2,0,1:T(8,128)S(1)} fusion(f32[16,128,256]{2,0,1:T(8,128)S(1)} %copy-done, f32[60,128,256]{2,1,0:T(8,128)S(1)} %fusion.28, pred[]{:T(512)S(6)} %compare.3, s32[60]{0:T(128)S(1)} %dynamic_slice.31, pred[60]{0:T(512)(128)(4,1)S(1)} %dynamic_slice.32), kind=kOutput, calls=%fused_computation.4.clone.1 | convolution fusion | flops 378537856 | bytes 12058925 | tf_op jit(solution)/shard_map/while/body/eval_jaxpr/ndq,nb->bdq/dot_general | solution.py:36
  135.5 1.3 copy-done.1
  138.8 0.8 compare_and_fusion.2
  139.6 2.2 gather_fusion
  141.8 2.6 %fusion.28 = f32[60,128,256]{2,1,0:T(8,128)S(1)} fusion(bf16[60,256,64]{1,2,0:T(8,128)(2,1)S(1)} %gather_fusion, pred[60]{0:T(512)(128)(4,1)S(1)} %get-tuple-element.152, bf16[240,64,128]{2,1,0:T(8,128)(2,1)} %get-tuple-element.182, s32[]{:T(128)S(6)} %select_n.28), kind=kOutput, calls=%fused_computation.5.clone.1 | convolution fusion | flops 252641280 | bytes 10813504 | tf_op jit(solution)/shard_map/while/body/eval_jaxpr/qnk,nkd->ndq/dot_general | solution.py:32
  144.5 7.9 %select_add_fusion.2 = f32[16,128,256]{2,0,1:T(8,128)S(1)} fusion(f32[16,128,256]{2,0,1:T(8,128)S(1)} %copy-done, f32[60,128,256]{2,1,0:T(8,128)S(1)} %fusion.28, pred[]{:T(512)S(6)} %compare.3, s32[60]{0:T(128)S(1)} %dynamic_slice.31, pred[60]{0:T(512)(128)(4,1)S(1)} %dynamic_slice.32), kind=kOutput, calls=%fused_computation.4.clone.1 | convolution fusion | flops 378537856 | bytes 12058925 | tf_op jit(solution)/shard_map/while/body/eval_jaxpr/ndq,nb->bdq/dot_general | solution.py:36
  152.4 1.3 copy-done.1
  153.7 4.1 %copy.8 = f32[16,128,256]{2,1,0:T(8,128)} copy(f32[16,128,256]{2,0,1:T(8,128)} %get-tuple-element.52) | data formatting | bytes 4194304 | tf_op jit(solution)/shard_map/while | solution.py:40
  157.8 71.2 %reduce-scatter.2.cloned.1.call-done = f32[128,256]{1,0:T(8,128)} async-done(((f32[2048,256]{1,0:T(8,128)}), f32[128,256]{1,0:T(8,128)}) %reduce-scatter.2.cloned.1.call-update) | async-done | bytes 131088 | tf_op jit(solution)/shard_map/reduce_scatter | solution.py:42
  229.0 1.9 collective-permute-start
  230.9 1.5 collective-permute-done
  232.5 0.9 add.31
  233.4 3.3 %collective-permute-start.1 = (f32[128,256]{1,0:T(8,128)S(1)}, f32[128,256]{1,0:T(8,128)S(1)}, u32[]{:S(2)}, u32[]{:S(2)}) collective-permute-start(f32[128,256]{1,0:T(8,128)S(1)} %add.31), channel_id=1, source_target_pairs={{0,128},{64,192},{128,0},{192,64},{256,384},{320,448},{384,256},{4... | collective-permute-start | bytes 393224 | tf_op jit(solution)/shard_map/ppermute | solution.py:45
  236.7 4.2 %collective-permute-done.1 = f32[128,256]{1,0:T(8,128)S(1)} collective-permute-done((f32[128,256]{1,0:T(8,128)S(1)}, f32[128,256]{1,0:T(8,128)S(1)}, u32[]{:S(2)}, u32[]{:S(2)}) %collective-permute-start.1) | collective-permute-done | bytes 131104 | tf_op jit(solution)/shard_map/ppermute | solution.py:45
  240.9 4.8 %collective-permute-start.2 = (f32[128,256]{1,0:T(8,128)S(1)}, f32[128,256]{1,0:T(8,128)S(1)}, u32[]{:S(2)}, u32[]{:S(2)}) collective-permute-start(f32[128,256]{1,0:T(8,128)S(1)} %add.32), channel_id=1, source_target_pairs={{0,256},{64,320},{128,384},{192,448},{256,0},{320,64},{384,128},{4... | collective-permute-start | bytes 393224 | tf_op jit(solution)/shard_map/ppermute | solution.py:45
  245.7 3.6 %collective-permute-done.2 = f32[128,256]{1,0:T(8,128)S(1)} collective-permute-done((f32[128,256]{1,0:T(8,128)S(1)}, f32[128,256]{1,0:T(8,128)S(1)}, u32[]{:S(2)}, u32[]{:S(2)}) %collective-permute-start.2) | collective-permute-done | bytes 131104 | tf_op jit(solution)/shard_map/ppermute | solution.py:45
  (36 shorter events, 6.4 us)
Async XLA Ops:
  6.5 79.7 %all-gather.2.cloned.1.call-start = ((), (), s32[]{:S(2)}) async-start(), calls=%async_computation.1 | async-start | bytes 2088960 | tf_op jit(solution)/shard_map/all_gather | solution.py:16
  7.3 221.8 %reduce-scatter.2.cloned.1.call-start = ((), (), s32[]{:S(2)}) async-start(), calls=%async_computation.2 | async-start | bytes 2228224 | tf_op jit(solution)/shard_map/reduce_scatter | solution.py:42
  91.2 2.6 %copy-start = (f32[16,128,256]{2,0,1:T(8,128)S(1)}, f32[16,128,256]{2,0,1:T(8,128)}, u32[]{:S(2)}) copy-start(f32[16,128,256]{2,0,1:T(8,128)} %get-tuple-element.166) | copy-start | bytes 6291460 | tf_op jit(solution)/shard_map/while
  101.8 1.3 copy-start.1
  108.1 2.6 %copy-start = (f32[16,128,256]{2,0,1:T(8,128)S(1)}, f32[16,128,256]{2,0,1:T(8,128)}, u32[]{:S(2)}) copy-start(f32[16,128,256]{2,0,1:T(8,128)} %get-tuple-element.166) | copy-start | bytes 6291460 | tf_op jit(solution)/shard_map/while
  118.6 1.3 copy-start.1
  125.0 2.6 %copy-start = (f32[16,128,256]{2,0,1:T(8,128)S(1)}, f32[16,128,256]{2,0,1:T(8,128)}, u32[]{:S(2)}) copy-start(f32[16,128,256]{2,0,1:T(8,128)} %get-tuple-element.166) | copy-start | bytes 6291460 | tf_op jit(solution)/shard_map/while
  135.5 1.3 copy-start.1
  141.8 2.6 %copy-start = (f32[16,128,256]{2,0,1:T(8,128)S(1)}, f32[16,128,256]{2,0,1:T(8,128)}, u32[]{:S(2)}) copy-start(f32[16,128,256]{2,0,1:T(8,128)} %get-tuple-element.166) | copy-start | bytes 6291460 | tf_op jit(solution)/shard_map/while
  152.4 1.3 copy-start.1
  229.0 3.4 %collective-permute-start = (f32[128,256]{1,0:T(8,128)}, f32[128,256]{1,0:T(8,128)S(1)}, u32[]{:S(2)}, u32[]{:S(2)}) collective-permute-start(f32[128,256]{1,0:T(8,128)} %reduce-scatter.2.cloned.1.call-done), channel_id=1, source_target_pairs={{0,64},{64,0},{128,192},{192,128},{256,320},{320,256},{384,448},{4... | collective-permute-start | bytes 393224 | tf_op jit(solution)/shard_map/ppermute | solution.py:45
  233.4 7.4 %collective-permute-start.1 = (f32[128,256]{1,0:T(8,128)S(1)}, f32[128,256]{1,0:T(8,128)S(1)}, u32[]{:S(2)}, u32[]{:S(2)}) collective-permute-start(f32[128,256]{1,0:T(8,128)S(1)} %add.31), channel_id=1, source_target_pairs={{0,128},{64,192},{128,0},{192,64},{256,384},{320,448},{384,256},{4... | collective-permute-start | bytes 393224 | tf_op jit(solution)/shard_map/ppermute | solution.py:45
  240.9 8.4 %collective-permute-start.2 = (f32[128,256]{1,0:T(8,128)S(1)}, f32[128,256]{1,0:T(8,128)S(1)}, u32[]{:S(2)}, u32[]{:S(2)}) collective-permute-start(f32[128,256]{1,0:T(8,128)S(1)} %add.32), channel_id=1, source_target_pairs={{0,256},{64,320},{128,384},{192,448},{256,0},{320,64},{384,128},{4... | collective-permute-start | bytes 393224 | tf_op jit(solution)/shard_map/ppermute | solution.py:45
Sparse Core Ops, SparseCore 0:
  9.4 76.7 all-gather.1
  158.0 71.0 reduce-scatter.1
